TPU v7x, 32 devices: a whole 2x2x4 slice. The times are simulated.
32 devices in a mesh: view: 8 (over z, core), span: 4 (over y, x).
Axes of the slice: x: 2, y: 2, z: 4, core: 2. Of those that a mesh axis runs over, the one named last changes fastest.
Arguments:
- tokens: bfloat16 [8, 1024, 1024], P('view', 'span'), may hold values from -6 to 6
- scan_order: int32 [8, 1024], P('view'), may hold values from 0 to 1023, as said below
- w_merge: bfloat16 [4096, 1024], replicated, may hold values from -0.09375 to 0.09375
- bias: bfloat16 [1024], replicated, may hold values from -4 to 4
- cotangent: bfloat16 [8, 256, 1024], P('view', 'span'), may hold values from -6 to 6
Outputs:
- merged_out: bfloat16 [8, 256, 1024], P('view', 'span')
- token_grad: bfloat16 [8, 1024, 1024], P('view', 'span')
- weight_grad: float32 [4096, 1024], P(('view', 'span'))
- bias_grad: float32 [1024], replicated
Inputs may be any that keep to these rules, and one draw needn't show every extreme that they name: `scan_order`: each row is a permutation of the raster indices of one view. Call tokens 256 * b to 256 * (b + 1) - 1 band b, and scan positions 256 * c to 256 * (c + 1) - 1 block c: every block holds at most 96 tokens of any band, and in every row each block holds exactly 96 tokens of some band.
All inputs are finite; a program needn't handle non-finite values.
Results may differ from a plain program's by a relative error of at most 0.001.
Values may be sent and summed in bfloat16 or wider, within the bound.
No kernel may reach another device: no remote copies, remote signals or barrier semaphores. Data moves between devices by JAX's collectives and lax.ppermute only.
A program may use at most 128 MiB of HBM per device.

v0:
```python
import math
import jax
import jax.numpy as jnp
from jax import lax
from jax.sharding import PartitionSpec as P

COLS = 128


def body(tokens, scan_order, w_merge, bias, cotangent):
    spans = lax.axis_size("span")
    views = lax.axis_size("view")
    span_index = lax.axis_index("span")
    tok_dev = tokens.shape[1]
    width = tokens.shape[2]
    capacity = 3 * (tok_dev // spans) // 2
    rows_dev = tok_dev // COLS
    order_all = scan_order[0].reshape(spans, tok_dev)
    owners = order_all // tok_dev
    owner_hot = (owners[:, :, None] == jnp.arange(spans, dtype=jnp.int32)[None, None, :]).astype(
        jnp.int32
    )
    slot_rank = jnp.sum((jnp.cumsum(owner_hot, axis=1) - 1) * owner_hot, axis=2)
    dest_slots = owners * capacity + slot_rank
    my_slots = lax.dynamic_index_in_dim(dest_slots, span_index, 0, keepdims=False)
    outgoing = jnp.zeros((spans * capacity, width), jnp.bfloat16).at[my_slots].set(tokens[0])
    received = lax.all_to_all(
        outgoing.reshape(spans, capacity, width), "span", split_axis=0, concat_axis=0, tiled=True
    )
    arriving = owners == span_index
    source_slot = jnp.arange(spans, dtype=jnp.int32)[:, None] * capacity + slot_rank
    local_index = jnp.where(arriving, order_all - span_index * tok_dev, tok_dev)
    source_of = (
        jnp.zeros((tok_dev,), jnp.int32)
        .at[local_index.reshape(-1)]
        .set(source_slot.reshape(-1), mode="drop")
    )
    raster = received.reshape(spans * capacity, width)[source_of]
    merged = (
        raster.reshape(rows_dev // 2, 2, COLS // 2, 2, width)
        .transpose(0, 2, 1, 3, 4)
        .reshape(tok_dev // 4, 4 * width)
    )
    merged_out = (
        jnp.dot(merged, w_merge, preferred_element_type=jnp.float32) + bias.astype(jnp.float32)
    ).astype(jnp.bfloat16)
    grads = cotangent[0]
    grad_merged = lax.dot_general(
        grads, w_merge, (((1,), (1,)), ((), ())), preferred_element_type=jnp.float32
    ).astype(jnp.bfloat16)
    grad_raster = (
        grad_merged.reshape(rows_dev // 2, COLS // 2, 2, 2, width)
        .transpose(0, 2, 1, 3, 4)
        .reshape(tok_dev, width)
    )
    going_back = jnp.zeros((spans * capacity, width), jnp.bfloat16).at[source_of].set(grad_raster)
    returned = lax.all_to_all(
        going_back.reshape(spans, capacity, width), "span", split_axis=0, concat_axis=0, tiled=True
    )
    token_grad = returned.reshape(spans * capacity, width)[my_slots]
    kernel_rows = 4 * width
    merged_rows = merged.shape[0]
    group_rows = kernel_rows // (views * spans)
    regrouped = merged.reshape(merged_rows, views, spans, group_rows).transpose(0, 2, 1, 3)
    view_tokens = lax.all_to_all(regrouped, "span", split_axis=1, concat_axis=0, tiled=True)
    view_tokens = view_tokens.reshape(spans * merged_rows, views * group_rows)
    all_grads = lax.all_gather(grads, "span", axis=0, tiled=True)
    partial_sum = lax.dot_general(
        view_tokens, all_grads, (((0,), (0,)), ((), ())), preferred_element_type=jnp.float32
    )
    weight_sum = lax.psum_scatter(partial_sum, "view", scatter_dimension=0, tiled=True)
    bias_total = lax.psum(jnp.sum(grads.astype(jnp.float32), axis=0), ("view", "span"))
    grad_scale = 1.0 / math.sqrt(views * spans * (tok_dev // 4))
    return (merged_out[None], token_grad[None], weight_sum * grad_scale, bias_total * grad_scale)


def solution(mesh):
    in_specs = (P("view", "span", None), P("view", None), P(), P(), P("view", "span", None))
    out_specs = (P("view", "span", None), P("view", "span", None), P(("view", "span"), None), P())
    return jax.shard_map(body, mesh=mesh, in_specs=in_specs, out_specs=out_specs, check_vma=False)
```

profile of v0, /device:TPU:0, one launch (start us, length us, event | category | flops | bytes accessed | tf_op | source)
XLA Modules:
  0.0 131.2 jit_solution(6496516762859729099)
XLA Ops:
  7.2 0.8 and_select_fusion.1
  8.0 4.8 %reduce-window.6 = s32[4,4,2,128]{3,2,1,0:T(2,128)S(1)} reduce-window(s32[4,4,2,128]{3,2,1,0:T(2,128)S(1)} %compare_convert_fusion, s32[]{:T(128)} %constant.19.clone.1), window={size=1x1x1x128 pad=0_0x0_0x0_0x127_0}, to_apply=%region_0.1 | reduce-window | flops 520192 | bytes 32772 | tf_op jit(solution)/shard_map/reduce-window
  12.9 0.1 copy.16
  13.0 0.1 copy.17
  13.2 0.1 add_add_fusion
  13.3 0.5 broadcast.237
  13.8 1.3 %reduce.3 = s32[1024]{0:T(1024)S(1)} reduce(s32[1,1024]{1,0:T(1,128)} %param.6, s32[]{:T(128)} %broadcast.237), dimensions={0}, to_apply=%param.6.reduce_sub_computation.3 | reduce | bytes 8196 | tf_op args[1]
  15.2 2.6 %scatter_custom_fusion = bf16[384,1024]{1,0:T(8,128)(2,1)} fusion(s32[256]{0:T(256)S(1)} %bitcast.75, bf16[1,256,1024]{2,1,0:T(8,128)(2,1)S(1)} %copy-done, bf16[]{:T(256)} %constant.15.clone.1), kind=kCustom, calls=%fused_computation.13 | custom fusion | bytes 1310722 | tf_op jit(solution)/shard_map/scatter | solution.py:26
  17.8 5.2 %all-to-all-start = ((bf16[4,96,1024]{2,1,0:T(8,128)(2,1)}), bf16[4,96,1024]{2,1,0:T(8,128)(2,1)S(1)}, u32[]{:S(2)}, u32[]{:S(2)}) async-start(bf16[4,96,1024]{2,1,0:T(8,128)(2,1)} %bitcast.6), calls=%async_computation | async-start | bytes 1572864 | tf_op jit(solution)/shard_map/all_to_all | solution.py:27
  23.1 0.7 compare_select_fusion
  23.8 4.3 %scatter_custom_fusion.1 = s32[256]{0:T(256)S(1)} fusion(s32[1024]{0:T(1024)S(1)} %bitcast.78, s32[1024]{0:T(1024)S(1)} %bitcast.77, s32[]{:T(128)} %constant.19.clone.1), kind=kCustom, calls=%fused_computation.59 | custom fusion | bytes 1028 | tf_op jit(solution)/shard_map/scatter | solution.py:36
  28.2 5.7 %all-to-all-done = bf16[4,96,1024]{2,1,0:T(8,128)(2,1)S(1)} async-done(((bf16[4,96,1024]{2,1,0:T(8,128)(2,1)}), bf16[4,96,1024]{2,1,0:T(8,128)(2,1)S(1)}, u32[]{:S(2)}, u32[]{:S(2)}) %all-to-all-start) | async-done | bytes 786464 | tf_op jit(solution)/shard_map/all_to_all | solution.py:27
  33.8 1.2 gather_fusion
  35.0 0.2 reshape.224
  35.2 0.4 copy.30
  35.6 0.3 reshape_reshape.3
  35.9 0.9 copy.20
  36.8 3.5 %all-to-all-start.2 = ((bf16[64,4,8,128]{3,2,0,1:T(8,128)(2,1)}), bf16[64,4,8,128]{3,2,0,1:T(8,128)(2,1)S(1)}, u32[]{:S(2)}, u32[]{:S(2)}) async-start(bf16[64,4,8,128]{3,2,0,1:T(8,128)(2,1)} %copy.20), calls=%async_computation.2 | async-start | bytes 1048576 | tf_op jit(solution)/shard_map/all_to_all | solution.py:65
  40.3 13.7 %all-gather = bf16[1,256,1024]{2,1,0:T(8,128)(2,1)S(1)} all-gather(bf16[1,64,1024]{2,1,0:T(8,128)(2,1)S(1)} %copy-done.1), channel_id=2, replica_groups=mesh['view'=8,'span'=4] {'span'}, dimensions={1}, use_global_device_ids=true | all-gather | bytes 655360 | tf_op jit(solution)/shard_map/all_gather | solution.py:67
  54.0 2.7 %fusion.2 = f32[1024,1024]{1,0:T(8,128)} fusion(bf16[32,8,8,128]{3,2,1,0:T(8,128)(2,1)S(1)} %bitcast.70, bf16[1,256,1024]{2,1,0:T(8,128)(2,1)S(1)} %all-gather), kind=kOutput, calls=%fused_computation.9 | convolution fusion | flops 536870912 | bytes 5242880 | tf_op jit(solution)/shard_map/dot_general | solution.py:68
  56.7 6.0 %convolution_convert_fusion = bf16[64,4096]{1,0:T(8,128)(2,1)S(1)} fusion(bf16[4096,1024]{1,0:T(8,128)(2,1)} %param.7, bf16[1,64,1024]{2,1,0:T(8,128)(2,1)S(1)} %copy-done.1), kind=kOutput, calls=%fused_computation.5 | convolution fusion | flops 537133056 | bytes 9043968 | tf_op jit(solution)/shard_map/dot_general | solution.py:48
  62.8 0.4 reshape.226
  63.1 0.4 copy.29
  63.5 0.2 reshape.267
  63.7 2.6 %scatter_custom_fusion.2 = bf16[384,1024]{1,0:T(8,128)(2,1)} fusion(s32[256]{0:T(256)S(1)} %compare_select_fusion.6, bf16[256,1024]{1,0:T(8,128)(2,1)S(1)} %reshape.267, bf16[]{:T(256)} %constant.15.clone.1), kind=kCustom, calls=%fused_computation.17 | custom fusion | bytes 786434 | tf_op jit(solution)/shard_map/scatter | solution.py:56
  66.3 3.5 %all-to-all-start.1 = ((bf16[4,96,1024]{2,1,0:T(8,128)(2,1)}), bf16[4,96,1024]{2,1,0:T(8,128)(2,1)S(1)}, u32[]{:S(2)}, u32[]{:S(2)}) async-start(bf16[4,96,1024]{2,1,0:T(8,128)(2,1)} %bitcast.14), calls=%async_computation.1 | async-start | bytes 1572864 | tf_op jit(solution)/shard_map/all_to_all | solution.py:57
  69.9 44.0 %psum.7 = f32[1024]{0:T(1024)S(1)} all-reduce(f32[1024]{0:T(1024)S(1)} %convert_reduce_fusion), channel_id=1, replica_groups=mesh['view'=8,'span'=4] {'view','span'}, use_global_device_ids=true, to_apply=%region_8.9 | all-reduce | flops 1024 | bytes 8192 | tf_op jit(solution)/shard_map/psum | solution.py:72
  113.8 0.6 broadcast_multiply_fusion.1
  114.4 0.4 reshape.225
  114.8 2.0 %gather_fusion.1 = bf16[256,1024]{1,0:T(8,128)(2,1)} fusion(bf16[384,1024]{1,0:T(8,128)(2,1)S(1)} %bitcast.67, s32[1024]{0:T(1024)S(1)} %pad_clamp_fusion), kind=kCustom, calls=%fused_computation.1 | custom fusion | bytes 1049600 | tf_op jit(solution)/shard_map/gather | solution.py:60
  116.8 5.6 %fusion.1 = bf16[1,64,1024]{2,1,0:T(8,128)(2,1)} fusion(bf16[64,4096]{1,0:T(8,128)(2,1)S(1)} %reshape.225, bf16[4096,1024]{1,0:T(8,128)(2,1)} %param.7, f32[1024]{0:T(1024)S(1)} %convert_element_type.18), kind=kOutput, calls=%fused_computation.8 | convolution fusion | flops 537001984 | bytes 9048064 | tf_op jit(solution)/shard_map/dot_general | solution.py:45
  122.4 1.9 %broadcast_multiply_fusion = f32[128,1024]{1,0:T(8,128)} fusion(f32[128,1024]{1,0:T(8,128)} %reduce-scatter.2.cloned.1.call-done), kind=kLoop, calls=%fused_computation.21 | loop fusion | flops 131072 | bytes 1048576 | tf_op jit(solution)/shard_map/mul | solution.py:74
  (28 shorter events, 0.4 us)
Async XLA Ops:
  7.2 8.1 %copy-start = (bf16[1,256,1024]{2,1,0:T(8,128)(2,1)S(1)}, bf16[1,256,1024]{2,1,0:T(8,128)(2,1)}, u32[]{:S(2)}) copy-start(bf16[1,256,1024]{2,1,0:T(8,128)(2,1)} %param.5) | copy-start | bytes 1572868
  7.2 33.1 %copy-start.1 = (bf16[1,64,1024]{2,1,0:T(8,128)(2,1)S(1)}, bf16[1,64,1024]{2,1,0:T(8,128)(2,1)}, u32[]{:S(2)}) copy-start(bf16[1,64,1024]{2,1,0:T(8,128)(2,1)} %param.9) | copy-start | bytes 393220
  17.8 16.0 %all-to-all-start = ((bf16[4,96,1024]{2,1,0:T(8,128)(2,1)}), bf16[4,96,1024]{2,1,0:T(8,128)(2,1)S(1)}, u32[]{:S(2)}, u32[]{:S(2)}) async-start(bf16[4,96,1024]{2,1,0:T(8,128)(2,1)} %bitcast.6), calls=%async_computation | async-start | bytes 1572864 | tf_op jit(solution)/shard_map/all_to_all | solution.py:27
  36.8 17.2 %all-to-all-start.2 = ((bf16[64,4,8,128]{3,2,0,1:T(8,128)(2,1)}), bf16[64,4,8,128]{3,2,0,1:T(8,128)(2,1)S(1)}, u32[]{:S(2)}, u32[]{:S(2)}) async-start(bf16[64,4,8,128]{3,2,0,1:T(8,128)(2,1)} %copy.20), calls=%async_computation.2 | async-start | bytes 1048576 | tf_op jit(solution)/shard_map/all_to_all | solution.py:65
  40.3 82.2 %reduce-scatter.2.cloned.1.call-start = ((), (), s32[]{:S(2)}) async-start(), calls=%async_computation.4 | async-start | bytes 4718592 | tf_op jit(solution)/shard_map/reduce_scatter | solution.py:71
  56.7 13.1 %copy-start.2 = (bf16[1024]{0:T(1024)(128)(2,1)S(1)}, bf16[1024]{0:T(1024)(128)(2,1)}, u32[]{:S(2)}) copy-start(bf16[1024]{0:T(1024)(128)(2,1)} %param.8) | copy-start | bytes 6148
  66.3 48.5 %all-to-all-start.1 = ((bf16[4,96,1024]{2,1,0:T(8,128)(2,1)}), bf16[4,96,1024]{2,1,0:T(8,128)(2,1)S(1)}, u32[]{:S(2)}, u32[]{:S(2)}) async-start(bf16[4,96,1024]{2,1,0:T(8,128)(2,1)} %bitcast.14), calls=%async_computation.1 | async-start | bytes 1572864 | tf_op jit(solution)/shard_map/all_to_all | solution.py:57
Sparse Core Ops, SparseCore 0:
  56.8 51.2 reduce-scatter.1
where the time goes:
time: 132 us; the launch traced here: 131 us
  blocking collectives  57.6 us (44%)
  local copies, waits for them, and re-layouts  16.6 us (13%)
  matrix products  14.3 us (11%)
  between operations  14.2 us (11%)
  starting transfers between devices  12.2 us (9%)
  other arithmetic  10.4 us (8%)
  waiting for transfers between devices  5.71 us (4%)
    psum x1, blocking collectives, body(): lax.psum(jnp.sum(grads.astype(jnp.float32), axis=0), ('view', 'span'))  44 us
    all_gather x1, blocking collectives, body(): all_grads = lax.all_gather(grads, 'span', axis=0, tiled=True)  13.7 us
    dot_general x1, matrix products, body(): lax.dot_general(grads, w_merge, (((1,), (1,)), ((), ())), preferred_eleme...  6.04 us
    all_to_all x1, waiting for transfers between devices, body(): lax.all_to_all(outgoing.reshape(spans, capacity, width), 'span', split_ax...  5.69 us
    dot_general x1, matrix products, body(): jnp.dot(merged, w_merge, preferred_element_type=jnp.float32)  5.61 us
    all_to_all x1, starting transfers between devices, body(): lax.all_to_all(outgoing.reshape(spans, capacity, width), 'span', split_ax...  5.19 us
    another operation x2, other arithmetic  4.84 us
    scatter x1, local copies, waits for them, and re-layouts, body(): source_of = jnp.zeros((tok_dev,), jnp.int32).at[local_index.reshape(-1)]....  4.3 us
  transfers between devices with their start and end apart: 4, of which 1 were waited for; matrix products, arithmetic and copies ran while one was open for 18% of the time, Pallas kernels for 0%

commit v1 on v0

--- a/solution.py
+++ b/solution.py
@@ -64,7 +64,15 @@
     regrouped = merged.reshape(merged_rows, views, spans, group_rows).transpose(0, 2, 1, 3)
     view_tokens = lax.all_to_all(regrouped, "span", split_axis=1, concat_axis=0, tiled=True)
     view_tokens = view_tokens.reshape(spans * merged_rows, views * group_rows)
-    all_grads = lax.all_gather(grads, "span", axis=0, tiled=True)
+    ways, here = (lax.axis_size("span"), lax.axis_index("span"))
+    grown, reach = (grads, 1)
+    while reach < ways:
+        theirs = lax.ppermute(grown, "span", [(d, d ^ reach) for d in range(ways)])
+        mine_first = jnp.concatenate([grown, theirs], axis=0)
+        theirs_first = jnp.concatenate([theirs, grown], axis=0)
+        grown = jnp.where(here & reach == 0, mine_first, theirs_first)
+        reach = 2 * reach
+    all_grads = grown
     partial_sum = lax.dot_general(
         view_tokens, all_grads, (((0,), (0,)), ((), ())), preferred_element_type=jnp.float32
     )

time: 132 us -> 132 us (level)
  blocking collectives: 57.6 us -> 45 us
  waiting for transfers between devices: 5.71 us -> 14.6 us
  starting transfers between devices: 12.2 us -> 16.2 us
    all_gather x1 -> x0, blocking collectives: 13.7 us -> none  [body(): all_grads = lax.all_gather(grads, 'span', axis=0, tiled=True)]
    ppermute x0 -> x2, waiting for transfers between devices: none -> 9.59 us  [body(): theirs = lax.ppermute(grown, 'span', [(d, d ^ reach) for d in range(ways)])]
    ppermute x0 -> x2, starting transfers between devices: none -> 4.01 us  [body(): theirs = lax.ppermute(grown, 'span', [(d, d ^ reach) for d in range(ways)])]
  transfers between devices with their start and end apart: 4 -> 6, of which waited for: 1 -> 2; matrix products, arithmetic and copies ran while one was open for 18% -> 20% of each run, Pallas kernels for 0% -> 0%
where the time goes in v1:
time: 132 us
  blocking collectives  45 us (34%)
  local copies, waits for them, and re-layouts  16.6 us (13%)
  starting transfers between devices  16.2 us (12%)
  waiting for transfers between devices  14.6 us (11%)
  matrix products  14.3 us (11%)
  between operations  14.3 us (11%)
  other arithmetic  10.5 us (8%)
    psum x1, blocking collectives, body(): lax.psum(jnp.sum(grads.astype(jnp.float32), axis=0), ('view', 'span'))  45 us
    ppermute x2, waiting for transfers between devices, body(): theirs = lax.ppermute(grown, 'span', [(d, d ^ reach) for d in range(ways)])  9.59 us
    dot_general x1, matrix products, body(): lax.dot_general(grads, w_merge, (((1,), (1,)), ((), ())), preferred_eleme...  6.04 us
    dot_general x1, matrix products, body(): jnp.dot(merged, w_merge, preferred_element_type=jnp.float32)  5.61 us
    all_to_all x1, starting transfers between devices, body(): lax.all_to_all(outgoing.reshape(spans, capacity, width), 'span', split_ax...  5.19 us
    all_to_all x1, waiting for transfers between devices, body(): lax.all_to_all(outgoing.reshape(spans, capacity, width), 'span', split_ax...  5.03 us
    another operation x2, other arithmetic  4.84 us
    scatter x1, local copies, waits for them, and re-layouts, body(): source_of = jnp.zeros((tok_dev,), jnp.int32).at[local_index.reshape(-1)]....  4.3 us
  transfers between devices with their start and end apart: 6, of which 2 were waited for; matrix products, arithmetic and copies ran while one was open for 20% of the time, Pallas kernels for 0%

profile of v1, /device:TPU:0, one launch (start us, length us, event | category | flops | bytes accessed | tf_op | source)
XLA Modules:
  0.0 131.5 jit_solution(13441503164099892250)
XLA Ops:
  7.2 0.8 and_select_fusion.1
  8.0 4.8 %reduce-window.6 = s32[4,4,2,128]{3,2,1,0:T(2,128)S(1)} reduce-window(s32[4,4,2,128]{3,2,1,0:T(2,128)S(1)} %compare_convert_fusion, s32[]{:T(128)} %constant.17.clone.1), window={size=1x1x1x128 pad=0_0x0_0x0_0x127_0}, to_apply=%region_0.1 | reduce-window | flops 520192 | bytes 32772 | tf_op jit(solution)/shard_map/reduce-window
  12.9 0.1 copy.16
  13.3 0.5 broadcast.237
  13.8 1.3 %reduce.3 = s32[1024]{0:T(1024)S(1)} reduce(s32[1,1024]{1,0:T(1,128)} %param.6, s32[]{:T(128)} %broadcast.237), dimensions={0}, to_apply=%param.6.reduce_sub_computation.3 | reduce | bytes 8196 | tf_op args[1]
  15.2 2.6 %scatter_custom_fusion = bf16[384,1024]{1,0:T(8,128)(2,1)} fusion(s32[256]{0:T(256)S(1)} %bitcast.74, bf16[1,256,1024]{2,1,0:T(8,128)(2,1)S(1)} %copy-done, bf16[]{:T(256)} %constant.15.clone.1), kind=kCustom, calls=%fused_computation.18 | custom fusion | bytes 1310722 | tf_op jit(solution)/shard_map/scatter | solution.py:26
  17.8 5.2 %all-to-all-start = ((bf16[4,96,1024]{2,1,0:T(8,128)(2,1)}), bf16[4,96,1024]{2,1,0:T(8,128)(2,1)S(1)}, u32[]{:S(2)}, u32[]{:S(2)}) async-start(bf16[4,96,1024]{2,1,0:T(8,128)(2,1)} %bitcast.6), calls=%async_computation | async-start | bytes 1572864 | tf_op jit(solution)/shard_map/all_to_all | solution.py:27
  23.0 2.0 %collective-permute-start = (bf16[64,1024]{1,0:T(8,128)(2,1)}, bf16[64,1024]{1,0:T(8,128)(2,1)S(1)}, u32[]{:S(2)}, u32[]{:S(2)}) collective-permute-start(bf16[64,1024]{1,0:T(8,128)(2,1)} %bitcast.70), channel_id=1, source_target_pairs={{0,1},{1,0},{2,3},{3,2},{4,5},{5,4},{6,7},{7,6},{8,9},{9,8},{10,11... | collective-permute-start | bytes 393224 | tf_op jit(solution)/shard_map/ppermute | solution.py:70
  25.1 0.7 compare_select_fusion
  25.8 4.3 %scatter_custom_fusion.1 = s32[256]{0:T(256)S(1)} fusion(s32[1024]{0:T(1024)S(1)} %bitcast.77, s32[1024]{0:T(1024)S(1)} %bitcast.76, s32[]{:T(128)} %constant.17.clone.1), kind=kCustom, calls=%fused_computation.65 | custom fusion | bytes 1028 | tf_op jit(solution)/shard_map/scatter | solution.py:36
  30.2 5.0 %all-to-all-done = bf16[4,96,1024]{2,1,0:T(8,128)(2,1)S(1)} async-done(((bf16[4,96,1024]{2,1,0:T(8,128)(2,1)}), bf16[4,96,1024]{2,1,0:T(8,128)(2,1)S(1)}, u32[]{:S(2)}, u32[]{:S(2)}) %all-to-all-start) | async-done | bytes 786464 | tf_op jit(solution)/shard_map/all_to_all | solution.py:27
  35.2 1.2 gather_fusion
  36.4 0.2 reshape.224
  36.6 0.4 copy.30
  37.0 0.3 reshape_reshape.3
  37.3 0.9 copy.20
  38.2 3.5 %all-to-all-start.2 = ((bf16[64,4,8,128]{3,2,0,1:T(8,128)(2,1)}), bf16[64,4,8,128]{3,2,0,1:T(8,128)(2,1)S(1)}, u32[]{:S(2)}, u32[]{:S(2)}) async-start(bf16[64,4,8,128]{3,2,0,1:T(8,128)(2,1)} %copy.20), calls=%async_computation.2 | async-start | bytes 1048576 | tf_op jit(solution)/shard_map/all_to_all | solution.py:65
  41.8 2.0 %collective-permute-start.1 = (bf16[128,1024]{1,0:T(8,128)(2,1)S(1)}, bf16[128,1024]{1,0:T(8,128)(2,1)S(1)}, u32[]{:S(2)}, u32[]{:S(2)}) collective-permute-start(bf16[128,1024]{1,0:T(8,128)(2,1)S(1)} %maximum_select_fusion.2), channel_id=1, source_target_pairs={{0,2},{1,3},{2,0},{3,1},{4,6},{5,7},{6,4},{7,5},{8,10},{9,11},{10,... | collective-permute-start | bytes 786440 | tf_op jit(solution)/shard_map/ppermute | solution.py:70
  43.8 9.6 %collective-permute-done.1 = bf16[128,1024]{1,0:T(8,128)(2,1)S(1)} collective-permute-done((bf16[128,1024]{1,0:T(8,128)(2,1)S(1)}, bf16[128,1024]{1,0:T(8,128)(2,1)S(1)}, u32[]{:S(2)}, u32[]{:S(2)}) %collective-permute-start.1) | collective-permute-done | bytes 262176 | tf_op jit(solution)/shard_map/ppermute | solution.py:70
  53.3 2.7 %fusion.2 = f32[1024,1024]{1,0:T(8,128)} fusion(bf16[32,8,8,128]{3,2,1,0:T(8,128)(2,1)S(1)} %bitcast.67, bf16[128,1024]{1,0:T(8,128)(2,1)S(1)} %collective-permute-done.1, bf16[128,1024]{1,0:T(8,128)(2,1)S(1)} %maximum_select_fusion.2, pred[]{:T(512)S(6)} %eq.49), kind=kOutput, calls=%fused_computation.9 | convolution fusion | flops 539230208 | bytes 5242881 | tf_op jit(solution)/shard_map/dot_general | solution.py:76
  56.1 6.0 %convolution_convert_fusion = bf16[64,4096]{1,0:T(8,128)(2,1)S(1)} fusion(bf16[4096,1024]{1,0:T(8,128)(2,1)} %param.7, bf16[1,64,1024]{2,1,0:T(8,128)(2,1)S(1)} %copy-done.1), kind=kOutput, calls=%fused_computation.5 | convolution fusion | flops 537133056 | bytes 9043968 | tf_op jit(solution)/shard_map/dot_general | solution.py:48
  62.1 0.4 reshape.226
  62.5 0.4 copy.29
  62.9 0.2 reshape.267
  63.1 2.6 %scatter_custom_fusion.2 = bf16[384,1024]{1,0:T(8,128)(2,1)} fusion(s32[256]{0:T(256)S(1)} %compare_select_fusion.6, bf16[256,1024]{1,0:T(8,128)(2,1)S(1)} %reshape.267, bf16[]{:T(256)} %constant.15.clone.1), kind=kCustom, calls=%fused_computation.23 | custom fusion | bytes 786434 | tf_op jit(solution)/shard_map/scatter | solution.py:56
  65.7 3.5 %all-to-all-start.1 = ((bf16[4,96,1024]{2,1,0:T(8,128)(2,1)}), bf16[4,96,1024]{2,1,0:T(8,128)(2,1)S(1)}, u32[]{:S(2)}, u32[]{:S(2)}) async-start(bf16[4,96,1024]{2,1,0:T(8,128)(2,1)} %bitcast.14), calls=%async_computation.1 | async-start | bytes 1572864 | tf_op jit(solution)/shard_map/all_to_all | solution.py:57
  69.2 45.0 %psum.7 = f32[1024]{0:T(1024)S(1)} all-reduce(f32[1024]{0:T(1024)S(1)} %convert_reduce_fusion), channel_id=1, replica_groups=mesh['view'=8,'span'=4] {'view','span'}, use_global_device_ids=true, to_apply=%region_8.9 | all-reduce | flops 1024 | bytes 8192 | tf_op jit(solution)/shard_map/psum | solution.py:80
  114.2 0.6 broadcast_multiply_fusion.1
  114.8 0.4 reshape.225
  115.2 2.0 %gather_fusion.1 = bf16[256,1024]{1,0:T(8,128)(2,1)} fusion(bf16[384,1024]{1,0:T(8,128)(2,1)S(1)} %bitcast.64, s32[1024]{0:T(1024)S(1)} %pad_clamp_fusion), kind=kCustom, calls=%fused_computation.1 | custom fusion | bytes 1049600 | tf_op jit(solution)/shard_map/gather | solution.py:60
  117.2 5.6 %fusion.1 = bf16[1,64,1024]{2,1,0:T(8,128)(2,1)} fusion(bf16[64,4096]{1,0:T(8,128)(2,1)S(1)} %reshape.225, bf16[4096,1024]{1,0:T(8,128)(2,1)} %param.7, f32[1024]{0:T(1024)S(1)} %convert_element_type.18), kind=kOutput, calls=%fused_computation.8 | convolution fusion | flops 537001984 | bytes 9048064 | tf_op jit(solution)/shard_map/dot_general | solution.py:45
  122.8 1.9 %broadcast_multiply_fusion = f32[128,1024]{1,0:T(8,128)} fusion(f32[128,1024]{1,0:T(8,128)} %reduce-scatter.2.cloned.1.call-done), kind=kLoop, calls=%fused_computation.28 | loop fusion | flops 131072 | bytes 1048576 | tf_op jit(solution)/shard_map/mul | solution.py:82
  (32 shorter events, 0.6 us)
Async XLA Ops:
  7.2 8.1 %copy-start = (bf16[1,256,1024]{2,1,0:T(8,128)(2,1)S(1)}, bf16[1,256,1024]{2,1,0:T(8,128)(2,1)}, u32[]{:S(2)}) copy-start(bf16[1,256,1024]{2,1,0:T(8,128)(2,1)} %param.5) | copy-start | bytes 1572868
  7.2 34.5 %copy-start.1 = (bf16[1,64,1024]{2,1,0:T(8,128)(2,1)S(1)}, bf16[1,64,1024]{2,1,0:T(8,128)(2,1)}, u32[]{:S(2)}) copy-start(bf16[1,64,1024]{2,1,0:T(8,128)(2,1)} %param.9) | copy-start | bytes 393220
  17.8 17.4 %all-to-all-start = ((bf16[4,96,1024]{2,1,0:T(8,128)(2,1)}), bf16[4,96,1024]{2,1,0:T(8,128)(2,1)S(1)}, u32[]{:S(2)}, u32[]{:S(2)}) async-start(bf16[4,96,1024]{2,1,0:T(8,128)(2,1)} %bitcast.6), calls=%async_computation | async-start | bytes 1572864 | tf_op jit(solution)/shard_map/all_to_all | solution.py:27
  23.0 18.7 %collective-permute-start = (bf16[64,1024]{1,0:T(8,128)(2,1)}, bf16[64,1024]{1,0:T(8,128)(2,1)S(1)}, u32[]{:S(2)}, u32[]{:S(2)}) collective-permute-start(bf16[64,1024]{1,0:T(8,128)(2,1)} %bitcast.70), channel_id=1, source_target_pairs={{0,1},{1,0},{2,3},{3,2},{4,5},{5,4},{6,7},{7,6},{8,9},{9,8},{10,11... | collective-permute-start | bytes 393224 | tf_op jit(solution)/shard_map/ppermute | solution.py:70
  38.2 15.2 %all-to-all-start.2 = ((bf16[64,4,8,128]{3,2,0,1:T(8,128)(2,1)}), bf16[64,4,8,128]{3,2,0,1:T(8,128)(2,1)S(1)}, u32[]{:S(2)}, u32[]{:S(2)}) async-start(bf16[64,4,8,128]{3,2,0,1:T(8,128)(2,1)} %copy.20), calls=%async_computation.2 | async-start | bytes 1048576 | tf_op jit(solution)/shard_map/all_to_all | solution.py:65
  41.6 81.2 %reduce-scatter.2.cloned.1.call-start = ((), (), s32[]{:S(2)}) async-start(), calls=%async_computation.4 | async-start | bytes 4718592 | tf_op jit(solution)/shard_map/reduce_scatter | solution.py:79
  41.8 11.6 %collective-permute-start.1 = (bf16[128,1024]{1,0:T(8,128)(2,1)S(1)}, bf16[128,1024]{1,0:T(8,128)(2,1)S(1)}, u32[]{:S(2)}, u32[]{:S(2)}) collective-permute-start(bf16[128,1024]{1,0:T(8,128)(2,1)S(1)} %maximum_select_fusion.2), channel_id=1, source_target_pairs={{0,2},{1,3},{2,0},{3,1},{4,6},{5,7},{6,4},{7,5},{8,10},{9,11},{10,... | collective-permute-start | bytes 786440 | tf_op jit(solution)/shard_map/ppermute | solution.py:70
  56.0 13.1 %copy-start.2 = (bf16[1024]{0:T(1024)(128)(2,1)S(1)}, bf16[1024]{0:T(1024)(128)(2,1)}, u32[]{:S(2)}) copy-start(bf16[1024]{0:T(1024)(128)(2,1)} %param.8) | copy-start | bytes 6148
  65.7 49.6 %all-to-all-start.1 = ((bf16[4,96,1024]{2,1,0:T(8,128)(2,1)}), bf16[4,96,1024]{2,1,0:T(8,128)(2,1)S(1)}, u32[]{:S(2)}, u32[]{:S(2)}) async-start(bf16[4,96,1024]{2,1,0:T(8,128)(2,1)} %bitcast.14), calls=%async_computation.1 | async-start | bytes 1572864 | tf_op jit(solution)/shard_map/all_to_all | solution.py:57
Sparse Core Ops, SparseCore 0:
  56.2 51.2 reduce-scatter.1
